TPU v7x, 32 devices: a whole 2x2x4 slice. The times are simulated.
32 devices in a mesh: img: 8 (over z, core), txt: 4 (over y, x).
Axes of the slice: x: 2, y: 2, z: 4, core: 2. Of those that a mesh axis runs over, the one named last changes fastest.
Arguments:
- image_emb: float32 [1024, 1536], P('img', 'txt'), may hold values from -0.15625 to 0.15625
- text_emb: float32 [1024, 1536], P('txt', 'img'), may hold values from -0.15625 to 0.15625
- vision_feat: bfloat16 [1024, 5120], P('img', 'txt'), may hold values from -0.125 to 0.125
- positive: int32 [1024], P('img'), may hold values from 0 to 1023, each once
- logit_scale: float32 [1], replicated, may hold values from 5 to 15
- logit_bias: float32 [1], replicated, may hold values from -3 to -1
Outputs:
- grad_image: float32 [1024, 1536], P('img', 'txt')
- grad_text: float32 [1024, 1536], P('txt', 'img')
- grad_proj: float32 [5120, 1536], P('txt', 'img')
Inputs may be any that keep to these rules, and one draw needn't show every extreme that they name: `positive`: each text index is the match of exactly one image.
All inputs are finite; a program needn't handle non-finite values.
Results may differ from a plain program's by a relative error of at most 0.0029.
Values may be sent and summed in bfloat16 or wider, within the bound.
A program may use at most 64 MiB of HBM per device.

v0:
```python
import jax
import jax.numpy as jnp
from jax import lax
from jax.sharding import PartitionSpec as P


def per_device(image_emb, text_emb, vision_feat, positive, logit_scale, logit_bias):
    scale = logit_scale[0]
    bias = logit_bias[0]
    image_full = lax.all_gather(image_emb, "txt", axis=1, tiled=True)
    text_full = lax.all_gather(text_emb, "img", axis=1, tiled=True)
    text_rows = text_full.shape[0]
    first_col = lax.axis_index("txt") * text_rows
    columns = first_col + lax.iota(jnp.int32, text_rows)
    logits = (
        scale
        * jnp.dot(
            image_full,
            text_full.T,
            precision=lax.Precision.HIGHEST,
            preferred_element_type=jnp.float32,
        )
        + bias
    )
    sign = jnp.where(positive[:, None] == columns[None, :], 1.0, -1.0).astype(jnp.float32)
    slope = -sign * jax.nn.sigmoid(-sign * logits)
    image_terms = scale * jnp.dot(
        slope, text_full, precision=lax.Precision.HIGHEST, preferred_element_type=jnp.float32
    )
    text_terms = scale * jnp.dot(
        slope.T, image_full, precision=lax.Precision.HIGHEST, preferred_element_type=jnp.float32
    )
    grad_text = lax.psum_scatter(text_terms, "img", scatter_dimension=1, tiled=True)
    grad_image = lax.psum_scatter(image_terms, "txt", scatter_dimension=1, tiled=True)
    image_low = lax.all_gather(grad_image.astype(jnp.bfloat16), "txt", axis=1, tiled=True)
    weight_terms = jnp.dot(vision_feat.T, image_low, preferred_element_type=jnp.float32)
    grad_proj = lax.psum_scatter(weight_terms, "img", scatter_dimension=1, tiled=True)
    return (grad_image, grad_text, grad_proj)


def solution(mesh):
    placed = (P("img", "txt"), P("txt", "img"), P("img", "txt"), P("img"), P(), P())
    return jax.shard_map(
        per_device,
        mesh=mesh,
        in_specs=placed,
        out_specs=(P("img", "txt"), P("txt", "img"), P("txt", "img")),
        check_vma=False,
    )
```

profile of v0, /device:TPU:0, one launch (start us, length us, event | category | flops | bytes accessed | tf_op | source)
XLA Modules:
  0.0 197.5 jit_solution(13368164841383276758)
XLA Ops:
  7.2 0.0 copy-start
  7.2 0.0 all-gather.2.cloned.1.call-start
  7.2 0.7 all-gather.2.cloned.1.call-update
  7.9 0.0 reduce-scatter.4.cloned.1.call-start
  9.3 15.9 %all_gather.9 = f32[128,1536]{1,0:T(8,128)S(1)} all-gather(f32[128,384]{1,0:T(8,128)} %param.6), channel_id=1, replica_groups=mesh['img'=8,'txt'=4] {'txt'}, dimensions={1}, use_global_device_ids=true | all-gather | bytes 983040 | tf_op jit(solution)/shard_map/all_gather | solution.py:10
  25.2 12.5 %all-gather.2.cloned.1.call-done = f32[256,1536]{0,1:T(8,128)} async-done(((f32[256,192]{0,1:T(8,128)}), f32[256,1536]{0,1:T(8,128)}) %all-gather.2.cloned.1.call-update) | async-done | bytes 1572880 | tf_op jit(solution)/shard_map/all_gather | solution.py:11
  37.7 0.0 copy-start.1
  37.7 2.4 %fusion.6 = f32[128,256]{1,0:T(8,128)S(1)} fusion(f32[128,1536]{1,0:T(8,128)S(1)} %all_gather.9, f32[256,1536]{0,1:T(8,128)} %all-gather.2.cloned.1.call-done, f32[]{:T(128)} %bitcast.15, f32[]{:T(128)} %bitcast.13, s32[256]{0:T(256)S(1)} %iota_add_fusion, s32[128]{0:T(128)} %param.9), kind=kOutput, calls=%fused_computation.10 | convolution fusion | flops 604307456 | bytes 2491912 | tf_op jit(solution)/shard_map/dot_general | solution.py:17
  40.1 0.0 copy-done.1
  40.1 2.6 %convolution_multiply_fusion.1 = f32[128,1536]{1,0:T(8,128)} fusion(f32[128,256]{1,0:T(8,128)S(1)} %fusion.6, f32[256,1536]{0,1:T(8,128)S(1)} %copy-done.1, f32[]{:T(128)} %bitcast.12), kind=kOutput, calls=%fused_computation.2 | convolution fusion | flops 604176384 | bytes 2490372 | tf_op jit(solution)/shard_map/dot_general | solution.py:27
  42.7 0.0 reduce-scatter.4.cloned.1.call-update
  42.7 0.0 reduce-scatter.6.cloned.1.call-start
  42.8 2.7 %convolution_multiply_fusion = f32[256,1536]{0,1:T(8,128)} fusion(f32[128,256]{1,0:T(8,128)S(1)} %fusion.6, f32[128,1536]{1,0:T(8,128)S(1)} %all_gather.9, f32[]{:T(128)} %bitcast.14), kind=kOutput, calls=%fused_computation.1 | convolution fusion | flops 604372992 | bytes 2490372 | tf_op jit(solution)/shard_map/dot_general | solution.py:30
  45.4 0.0 reduce-scatter.6.cloned.1.call-update
  45.5 0.0 reduce-scatter.8.cloned.1.call-start
  45.5 22.7 %reduce-scatter.4.cloned.1.call-done = f32[128,384]{1,0:T(8,128)} async-done(((f32[128,1536]{1,0:T(8,128)}), f32[128,384]{1,0:T(8,128)}) %reduce-scatter.4.cloned.1.call-update) | async-done | bytes 196624 | tf_op jit(solution)/shard_map/reduce_scatter | solution.py:34
  68.2 0.9 convert_element_type.3
  69.1 10.1 %all_gather.11 = bf16[128,1536]{1,0:T(8,128)(2,1)S(1)} all-gather(bf16[128,384]{1,0:T(8,128)(2,1)S(1)} %convert_element_type.3), channel_id=1, replica_groups=mesh['img'=8,'txt'=4] {'txt'}, dimensions={1}, use_global_device_ids=true | all-gather | bytes 491520 | tf_op jit(solution)/shard_map/all_gather | solution.py:35
  79.2 0.0 copy-done
  79.2 4.3 %convolution_bitcast_fusion = f32[1280,1536]{0,1:T(8,128)} fusion(bf16[128,1536]{1,0:T(8,128)(2,1)S(1)} %all_gather.11, bf16[128,1280]{1,0:T(8,128)(2,1)S(1)} %copy-done), kind=kOutput, calls=%fused_computation | convolution fusion | flops 503316480 | bytes 8585216 | tf_op jit(solution)/shard_map/dot_general | solution.py:36
  83.5 0.0 reduce-scatter.8.cloned.1.call-update
  83.5 21.9 %reduce-scatter.6.cloned.1.call-done = f32[256,192]{0,1:T(8,128)} async-done(((f32[256,1536]{0,1:T(8,128)}), f32[256,192]{0,1:T(8,128)}) %reduce-scatter.6.cloned.1.call-update) | async-done | bytes 196624 | tf_op jit(solution)/shard_map/reduce_scatter | solution.py:33
  105.4 85.6 %reduce-scatter.8.cloned.1.call-done = f32[1280,192]{0,1:T(8,128)} async-done(((f32[1280,1536]{0,1:T(8,128)}), f32[1280,192]{0,1:T(8,128)}) %reduce-scatter.8.cloned.1.call-update) | async-done | bytes 983056 | tf_op jit(solution)/shard_map/reduce_scatter | solution.py:37
  (1 shorter events, 0.0 us)
Async XLA Ops:
  7.2 72.1 %copy-start = (bf16[128,1280]{1,0:T(8,128)(2,1)S(1)}, bf16[128,1280]{1,0:T(8,128)(2,1)}, u32[]{:S(2)}) copy-start(bf16[128,1280]{1,0:T(8,128)(2,1)} %param.8) | copy-start | bytes 983044
  7.2 30.5 %all-gather.2.cloned.1.call-start = ((), (), s32[]{:S(2)}) async-start(), calls=%async_computation.3 | async-start | bytes 1769472 | tf_op jit(solution)/shard_map/all_gather | solution.py:11
  7.9 60.3 %reduce-scatter.4.cloned.1.call-start = ((), (), s32[]{:S(2)}) async-start(), calls=%async_computation.4 | async-start | bytes 983040 | tf_op jit(solution)/shard_map/reduce_scatter | solution.py:34
  37.7 2.5 %copy-start.1 = (f32[256,1536]{0,1:T(8,128)S(1)}, f32[256,1536]{0,1:T(8,128)}, u32[]{:S(2)}) copy-start(f32[256,1536]{0,1:T(8,128)} %all-gather.2.cloned.1.call-done) | copy-start | bytes 4718596
  42.7 62.7 %reduce-scatter.6.cloned.1.call-start = ((), (), s32[]{:S(2)}) async-start(), calls=%async_computation.5 | async-start | bytes 1769472 | tf_op jit(solution)/shard_map/reduce_scatter | solution.py:33
  45.5 145.5 %reduce-scatter.8.cloned.1.call-start = ((), (), s32[]{:S(2)}) async-start(), calls=%async_computation.6 | async-start | bytes 8847360 | tf_op jit(solution)/shard_map/reduce_scatter | solution.py:37
Sparse Core Ops, SparseCore 0:
  9.6 27.9 all-gather.1
  42.9 25.2 reduce-scatter.3
  71.1 34.2 reduce-scatter.5
  108.1 82.8 reduce-scatter.7
where the time goes:
time: 198 us
  waiting for transfers between devices  143 us (72%)
  blocking collectives  26 us (13%)
  between operations  15.1 us (8%)
  matrix products  12 us (6%)
    reduce_scatter x1, waiting for transfers between devices, per_device(): lax.psum_scatter(weight_terms, 'img', scatter_dimension=1, tiled=True)  85.6 us
    reduce_scatter x1, waiting for transfers between devices, per_device(): lax.psum_scatter(image_terms, 'txt', scatter_dimension=1, tiled=True)  22.7 us
    reduce_scatter x1, waiting for transfers between devices, per_device(): lax.psum_scatter(text_terms, 'img', scatter_dimension=1, tiled=True)  21.9 us
    all_gather x1, blocking collectives, per_device(): image_full = lax.all_gather(image_emb, 'txt', axis=1, tiled=True)  15.9 us
    all_gather x1, waiting for transfers between devices, per_device(): text_full = lax.all_gather(text_emb, 'img', axis=1, tiled=True)  12.5 us
    all_gather x1, blocking collectives, per_device(): lax.all_gather(grad_image.astype(jnp.bfloat16), 'txt', axis=1, tiled=True)  10.1 us
    dot_general x1, matrix products, per_device(): jnp.dot(vision_feat.T, image_low, preferred_element_type=jnp.float32)  4.28 us
  transfers between devices with their start and end apart: 4, of which 4 were waited for; matrix products, arithmetic and copies ran while one was open for 4% of the time, Pallas kernels for 0%

commit v1 on v0

--- a/solution.py
+++ b/solution.py
@@ -8,7 +8,7 @@
     scale = logit_scale[0]
     bias = logit_bias[0]
     image_full = lax.all_gather(image_emb, "txt", axis=1, tiled=True)
-    text_full = lax.all_gather(text_emb, "img", axis=1, tiled=True)
+    text_full = jnp.concatenate(lax.all_gather(text_emb, "img"), axis=1)
     text_rows = text_full.shape[0]
     first_col = lax.axis_index("txt") * text_rows
     columns = first_col + lax.iota(jnp.int32, text_rows)

time: 198 us -> 199 us (level)
  local copies, waits for them, and re-layouts: 0.01 us -> 2.67 us
    unnamed x4 -> x5, local copies, waits for them, and re-layouts: 0.01 us -> 2.16 us
where the time goes in v1:
time: 199 us
  waiting for transfers between devices  143 us (72%)
  blocking collectives  26 us (13%)
  between operations  15.1 us (8%)
  matrix products  10.5 us (5%)
  local copies, waits for them, and re-layouts  2.67 us (1%)
    reduce_scatter x1, waiting for transfers between devices, per_device(): lax.psum_scatter(weight_terms, 'img', scatter_dimension=1, tiled=True)  85.7 us
    reduce_scatter x1, waiting for transfers between devices, per_device(): lax.psum_scatter(image_terms, 'txt', scatter_dimension=1, tiled=True)  22.7 us
    reduce_scatter x1, waiting for transfers between devices, per_device(): lax.psum_scatter(text_terms, 'img', scatter_dimension=1, tiled=True)  21.7 us
    all_gather x1, blocking collectives, per_device(): image_full = lax.all_gather(image_emb, 'txt', axis=1, tiled=True)  15.9 us
    all_gather x1, waiting for transfers between devices, per_device(): text_full = jnp.concatenate(lax.all_gather(text_emb, 'img'), axis=1)  12.4 us
    all_gather x1, blocking collectives, per_device(): lax.all_gather(grad_image.astype(jnp.bfloat16), 'txt', axis=1, tiled=True)  10.1 us
    dot_general x1, matrix products, per_device(): jnp.dot(vision_feat.T, image_low, preferred_element_type=jnp.float32)  4.28 us
  transfers between devices with their start and end apart: 4, of which 4 were waited for; matrix products, arithmetic and copies ran while one was open for 4% of the time, Pallas kernels for 0%

profile of v1, /device:TPU:0, one launch (start us, length us, event | category | flops | bytes accessed | tf_op | source)
XLA Modules:
  0.0 198.6 jit_solution(9986537019332091934)
XLA Ops:
  7.2 0.0 copy-start
  7.2 0.0 all-gather.3.cloned.1.call-start
  7.2 0.7 all-gather.3.cloned.1.call-update
  7.9 0.0 reduce-scatter.4.cloned.1.call-start
  9.3 15.9 %all_gather.12 = f32[128,1536]{1,0:T(8,128)S(1)} all-gather(f32[128,384]{1,0:T(8,128)} %param.6), channel_id=1, replica_groups=mesh['img'=8,'txt'=4] {'txt'}, dimensions={1}, use_global_device_ids=true | all-gather | bytes 983040 | tf_op jit(solution)/shard_map/all_gather | solution.py:10
  25.2 12.4 %all-gather.3.cloned.1.call-done = f32[2048,192]{0,1:T(8,128)} async-done(((f32[256,192]{0,1:T(8,128)}), f32[2048,192]{0,1:T(8,128)}) %all-gather.3.cloned.1.call-update) | async-done | bytes 1572880 | tf_op jit(solution)/shard_map/all_gather | solution.py:11
  37.6 2.0 %copy.10 = f32[24,8,8,256]{3,2,1,0:T(8,128)S(1)} copy(f32[24,8,8,256]{3,1,2,0:T(8,128)} %bitcast.26) | data formatting | bytes 3145728
  39.6 0.0 copy-start.1
  39.6 0.5 copy.9
  40.2 0.1 copy-done.1
  40.3 0.9 fusion.6
  41.2 2.6 %convolution_multiply_fusion.1 = f32[128,1536]{1,0:T(8,128)} fusion(f32[128,256]{1,0:T(8,128)S(1)} %fusion.6, f32[256,1536]{0,1:T(8,128)S(1)} %bitcast.24, f32[]{:T(128)} %bitcast.19), kind=kOutput, calls=%fused_computation.2 | convolution fusion | flops 604176384 | bytes 2490372 | tf_op jit(solution)/shard_map/dot_general | solution.py:27
  43.8 0.0 reduce-scatter.4.cloned.1.call-update
  43.8 0.0 reduce-scatter.6.cloned.1.call-start
  43.9 2.7 %convolution_multiply_fusion = f32[256,1536]{0,1:T(8,128)} fusion(f32[128,256]{1,0:T(8,128)S(1)} %fusion.6, f32[128,1536]{1,0:T(8,128)S(1)} %all_gather.12, f32[]{:T(128)} %bitcast.21), kind=kOutput, calls=%fused_computation.1 | convolution fusion | flops 604372992 | bytes 2490372 | tf_op jit(solution)/shard_map/dot_general | solution.py:30
  46.6 0.0 reduce-scatter.6.cloned.1.call-update
  46.6 0.0 reduce-scatter.8.cloned.1.call-start
  46.6 22.7 %reduce-scatter.4.cloned.1.call-done = f32[128,384]{1,0:T(8,128)} async-done(((f32[128,1536]{1,0:T(8,128)}), f32[128,384]{1,0:T(8,128)}) %reduce-scatter.4.cloned.1.call-update) | async-done | bytes 196624 | tf_op jit(solution)/shard_map/reduce_scatter | solution.py:34
  69.3 0.9 convert_element_type.3
  70.2 10.1 %all_gather.15 = bf16[128,1536]{1,0:T(8,128)(2,1)S(1)} all-gather(bf16[128,384]{1,0:T(8,128)(2,1)S(1)} %convert_element_type.3), channel_id=1, replica_groups=mesh['img'=8,'txt'=4] {'txt'}, dimensions={1}, use_global_device_ids=true | all-gather | bytes 491520 | tf_op jit(solution)/shard_map/all_gather | solution.py:35
  80.3 0.0 copy-done
  80.3 4.3 %convolution_bitcast_fusion = f32[1280,1536]{0,1:T(8,128)} fusion(bf16[128,1536]{1,0:T(8,128)(2,1)S(1)} %all_gather.15, bf16[128,1280]{1,0:T(8,128)(2,1)S(1)} %copy-done), kind=kOutput, calls=%fused_computation | convolution fusion | flops 503316480 | bytes 8585216 | tf_op jit(solution)/shard_map/dot_general | solution.py:36
  84.6 0.0 reduce-scatter.8.cloned.1.call-update
  84.6 21.7 %reduce-scatter.6.cloned.1.call-done = f32[256,192]{0,1:T(8,128)} async-done(((f32[256,1536]{0,1:T(8,128)}), f32[256,192]{0,1:T(8,128)}) %reduce-scatter.6.cloned.1.call-update) | async-done | bytes 196624 | tf_op jit(solution)/shard_map/reduce_scatter | solution.py:33
  106.4 85.7 %reduce-scatter.8.cloned.1.call-done = f32[1280,192]{0,1:T(8,128)} async-done(((f32[1280,1536]{0,1:T(8,128)}), f32[1280,192]{0,1:T(8,128)}) %reduce-scatter.8.cloned.1.call-update) | async-done | bytes 983056 | tf_op jit(solution)/shard_map/reduce_scatter | solution.py:37
  (1 shorter events, 0.0 us)
Async XLA Ops:
  7.2 73.2 %copy-start = (bf16[128,1280]{1,0:T(8,128)(2,1)S(1)}, bf16[128,1280]{1,0:T(8,128)(2,1)}, u32[]{:S(2)}) copy-start(bf16[128,1280]{1,0:T(8,128)(2,1)} %param.8) | copy-start | bytes 983044
  7.2 30.4 %all-gather.3.cloned.1.call-start = ((), (), s32[]{:S(2)}) async-start(), calls=%async_computation.6 | async-start | bytes 1769472 | tf_op jit(solution)/shard_map/all_gather | solution.py:11
  7.9 61.4 %reduce-scatter.4.cloned.1.call-start = ((), (), s32[]{:S(2)}) async-start(), calls=%async_computation.3 | async-start | bytes 983040 | tf_op jit(solution)/shard_map/reduce_scatter | solution.py:34
  39.6 0.7 copy-start.1
  43.8 62.5 %reduce-scatter.6.cloned.1.call-start = ((), (), s32[]{:S(2)}) async-start(), calls=%async_computation.4 | async-start | bytes 1769472 | tf_op jit(solution)/shard_map/reduce_scatter | solution.py:33
  46.6 145.5 %reduce-scatter.8.cloned.1.call-start = ((), (), s32[]{:S(2)}) async-start(), calls=%async_computation.5 | async-start | bytes 8847360 | tf_op jit(solution)/shard_map/reduce_scatter | solution.py:37
Sparse Core Ops, SparseCore 0:
  9.6 27.9 all-gather.2
  44.0 25.2 reduce-scatter.3
  72.2 34.1 reduce-scatter.5
  109.1 82.9 reduce-scatter.7
